TPU v7x, 256 devices: a whole 4x4x8 slice. The times are simulated.
256 devices in a mesh: md: 64 (over z_hi, x, y), th: 4 (over z_lo, core).
Axes of the slice: x: 4, y: 4, z: 8 (z_hi: 4, z_lo: 2; z = z_hi * 2 + z_lo), core: 2. Of those that a mesh axis runs over, the one named last changes fastest.
Arguments:
- populations: float32 [19, 128, 128, 512], P(None, 'md', 'th'), may hold values from 0.01 to 0.52, as said below
- fibre_mask: int32 [128, 128, 512], P('md', 'th'), may hold values 0 or 1
- wire_open: int32 [128, 512], P('md'), may hold values 0 or 1
- fines: float32 [4, 128, 128, 512], P(None, 'md', None, 'th'), may hold values from 0.2 to 2
- diffusivity: float32 [4], replicated, may hold values from 20 to 400
- retention: float32 [4], replicated, may hold values from 0.05 to 0.5
Outputs:
- populations_out: float32 [19, 128, 128, 512], P(None, 'md', 'th')
- fines_out: float32 [4, 128, 128, 512], P(None, 'md', None, 'th')
Inputs may be any that keep to these rules, and one draw needn't show every extreme that they name: `populations`: each population lies between 0.45 and 1.55 times its lattice weight.
All inputs are finite; a program needn't handle non-finite values. No bound on the sum of `fibre_mask` or of `wire_open` on one device may be relied on, other than what follows from the above.
Results may differ from a plain program's by a relative error of at most 0.0003.
Values sent between devices are 32-bit elements; how exact they have to be, the bound alone decides.
A program may use at most 64 MiB of HBM per device.

v0:
```python
import functools

import jax
import jax.numpy as jnp
from jax import lax
from jax.experimental import pallas as pl
from jax.experimental.pallas import tpu as pltpu
from jax.sharding import PartitionSpec as P

VELOCITIES = [
    (0, 0, 0), (1, 0, 0), (-1, 0, 0), (0, 1, 0), (0, -1, 0), (0, 0, 1), (0, 0, -1),
    (1, 1, 0), (-1, -1, 0), (1, -1, 0), (-1, 1, 0), (1, 0, 1), (-1, 0, -1), (1, 0, -1),
    (-1, 0, 1), (0, 1, 1), (0, -1, -1), (0, 1, -1), (0, -1, 1),
]
WEIGHTS = [1.0 / 3.0] + [1.0 / 18.0] * 6 + [1.0 / 36.0] * 12
OPPOSITE = [0, 2, 1, 4, 3, 6, 5, 8, 7, 10, 9, 12, 11, 14, 13, 16, 15, 18, 17]
RELAXATION = 1.6
INLET_DENSITY = 1.03
OUTLET_DENSITY = 0.97
LATERAL_DIFFUSION = 0.1

PLUS = [1, 7, 9, 11, 13]
MINUS = [2, 8, 10, 12, 14]
ZERO = [0, 3, 4, 5, 6, 15, 16, 17, 18]
SLOT = {i: k for k, i in enumerate(PLUS + MINUS + ZERO)}
UP = [5, 15, 18, 11, 14]
DOWN = [6, 16, 17, 12, 13]

MESH = pl.DeviceIdType.MESH
LANES = 128
NT = 4
TOP = 8


def moments(f):
    def add(items):
        items = list(items)
        while len(items) > 1:
            items = [a + b for a, b in zip(items[::2], items[1::2])] + (
                [items[-1]] if len(items) % 2 else []
            )
        return items[0]

    mass = add(f)
    flux = []
    for axis in range(3):
        plus = add([f[i] for i in range(19) if VELOCITIES[i][axis] == 1])
        minus = add([f[i] for i in range(19) if VELOCITIES[i][axis] == -1])
        flux.append(plus - minus)
    inverse = 1.0 / mass
    return mass, flux[0] * inverse, flux[1] * inverse, flux[2] * inverse


def collide(f, solid):
    mass, ux, uy, uz = moments(f)
    base = 1.0 - 1.5 * (ux * ux + uy * uy + uz * uz)
    out = [None] * 19
    out[0] = jnp.where(solid, f[0], (1.0 - RELAXATION) * f[0] + (RELAXATION * WEIGHTS[0]) * (mass * base))
    scaled = {w: (RELAXATION * w) * mass for w in (WEIGHTS[1], WEIGHTS[7])}
    for i in range(1, 19, 2):
        j = OPPOSITE[i]
        cx, cy, cz = VELOCITIES[i]
        terms = [u if c > 0 else -u for c, u in ((cx, ux), (cy, uy), (cz, uz)) if c != 0]
        p = functools.reduce(lambda a, b: a + b, terms)
        m = scaled[WEIGHTS[i]]
        even = m * (base + 4.5 * (p * p))
        odd = m * (3.0 * p)
        out[i] = jnp.where(solid, f[j], (1.0 - RELAXATION) * f[i] + (even + odd))
        out[j] = jnp.where(solid, f[i], (1.0 - RELAXATION) * f[j] + (even - odd))
    return out


def kernel(
    pops, mask, wire, fines, diff, ret, pops_out, fines_out,
    F, R, M, S, Sall, V, Vall, B, ZU, ZD, RU, RD, W, Q, C, X, G, YP, YW, YE,
    in_sem, out_sem, xs_s, xs_r, zs_s, zs_r, ss_s, ss_r, vs_s, vs_r, q_s, q_r, y_s, y_r,
):
    md = lax.axis_index("md")
    th = lax.axis_index("th")
    nmd = lax.axis_size("md")
    right, left = lax.rem(md + 1, nmd), lax.rem(md + nmd - 1, nmd)
    up, dn = lax.rem(th + 1, 4), lax.rem(th + 3, 4)
    peers = [lax.rem(th + d, 4) for d in (1, 2, 3)]

    loads = [
        pltpu.make_async_copy(fines, Q.at[0, :, 1:3, 8:136, :], in_sem.at[0]),
    ]
    for t in range(NT):
        loads.append(pltpu.make_async_copy(
            mask.at[:, :, t * LANES:(t + 1) * LANES], M.at[:, t], in_sem.at[1 + t]))
    for t in range(NT):
        loads.append(pltpu.make_async_copy(
            pops.at[:, :, :, t * LANES:(t + 1) * LANES], F.at[:, :, t], in_sem.at[5 + t]))
    for c in loads:
        c.start()

    barrier = pltpu.get_barrier_semaphore()
    friends = [(right, th), (left, th)] + [(md, p) for p in peers]
    friends += [(m, t) for m in (right, left) for t in (up, dn)]
    for d in friends:
        pl.semaphore_signal(barrier, inc=1, device_id=d, device_id_type=MESH)

    lane = lax.broadcasted_iota(jnp.int32, (8, LANES), 1)
    sub = lax.broadcasted_iota(jnp.int32, (8, LANES), 0)

    def remote(src, dst, s, r, dev):
        return pltpu.make_async_remote_copy(
            src_ref=src, dst_ref=dst, send_sem=s, recv_sem=r, device_id=dev, device_id_type=MESH)

    for x in range(2):
        for t in range(NT):
            W[x * NT + t:x * NT + t + 1, :] = wire[x:x + 1, t * LANES:(t + 1) * LANES]

    def pack_columns(buf, s, step):
        def body(k, carry):
            east, west = carry
            x, zc = k // 16, lax.rem(k, 16)
            c = Q[buf, s, x + 1, pl.ds(pl.multiple_of(8 + zc * 8, 8), 8), :]
            here = lane == k
            east = jnp.where(here, pltpu.roll(c, lax.rem(k + 1, LANES), 1), east)
            west = jnp.where(here, pltpu.roll(c, k, 1), west)
            return east, west
        zero = jnp.zeros((8, LANES), jnp.float32)
        east, west = lax.fori_loop(0, 32, body, (zero, zero))
        YP[step, s, 0] = east
        YP[step, s, 1] = west

    def fine_sends(step, s):
        return [
            remote(Q.at[step, s, 2, 8:136, :], Q.at[step, s, 0, 8:136, :], q_s.at[step, s, 0], q_r.at[step, s, 0], (right, th)),
            remote(Q.at[step, s, 1, 8:136, :], Q.at[step, s, 3, 8:136, :], q_s.at[step, s, 1], q_r.at[step, s, 1], (left, th)),
            remote(YP.at[step, s, 0], YW.at[step, s], y_s.at[step, s, 0], y_r.at[step, s, 0], (md, up)),
            remote(YP.at[step, s, 1], YE.at[step, s], y_s.at[step, s, 1], y_r.at[step, s, 1], (md, dn)),
        ]

    loads[0].wait()
    for s in range(4):
        pack_columns(0, s, 0)
    for t in range(NT):
        loads[1 + t].wait()
    S[...] = M[...].astype(jnp.float32)

    pl.semaphore_wait(barrier, len(friends))
    fine0 = [fine_sends(0, s) for s in range(4)]
    for s in range(4):
        for c in fine0[s]:
            c.start()
    my_rows = pl.ds(pl.multiple_of(th * 32, 32), 32)
    solids = [
        remote(S.at[:, p], Sall.at[:, my_rows, :], ss_s.at[k], ss_r.at[k], (md, p))
        for k, p in enumerate(peers)
    ]
    for c in solids:
        c.start()
    for x in range(2):
        Sall[x, my_rows, :] = S[x, th]

    def put(e, x, t, z, out):
        rows = pl.ds(pl.multiple_of(8 + z * 8, 8), 8)
        for i in range(19):
            cy = VELOCITIES[i][1]
            k = SLOT[i]
            if cy == 0:
                R[e, k, x + 1, t, rows, :] = out[i]
            elif cy == 1:
                v = pltpu.roll(out[i], 1, 1)
                R[e, k, x + 1, t, rows, 1:LANES] = v[:, 1:LANES]
                R[e, k, x + 1, lax.rem(t + 1, NT), rows, 0:1] = v[:, 0:1]
            else:
                v = pltpu.roll(out[i], LANES - 1, 1)
                R[e, k, x + 1, t, rows, 0:LANES - 1] = v[:, 0:LANES - 1]
                R[e, k, x + 1, lax.rem(t + 3, NT), rows, LANES - 1:LANES] = v[:, LANES - 1:LANES]
        for k in range(5):
            B[k, x * NT + t] = out[DOWN[k]]

    def solid_at(x, t, z):
        return S[x, t, pl.ds(pl.multiple_of(z * 8, 8), 8), :] > 0

    def chunks(body):
        def step(n, _):
            z = 3 - n // 8
            r = lax.rem(n, 8)
            body(r // NT, lax.rem(r, NT), z)
            return 0
        lax.fori_loop(0, 32, step, 0)

    def pull(e, x, t, z):
        f = []
        for i in range(19):
            cx, _, cz = VELOCITIES[i]
            f.append(R[e, SLOT[i], x + 1 - cx, t, pl.ds(8 + z * 8 - cz, 8), :])
        return f

    def exchange(e):
        for k in range(5):
            for x in range(2):
                for t in range(NT):
                    r = x * NT + t
                    ZU[e, k, r:r + 1, :] = R[e, SLOT[UP[k]], x + 1, t, 39:40, :]
                    ZD[e, k, r:r + 1, :] = R[e, SLOT[DOWN[k]], x + 1, t, 8:9, :]
        out = [
            remote(R.at[e, 0:5, 2, :, 8:40, :], R.at[e, 0:5, 0, :, 8:40, :], xs_s.at[e, 0], xs_r.at[e, 0], (right, th)),
            remote(R.at[e, 5:10, 1, :, 8:40, :], R.at[e, 5:10, 3, :, 8:40, :], xs_s.at[e, 1], xs_r.at[e, 1], (left, th)),
            remote(ZU.at[e], RU.at[e, 0:5], zs_s.at[e, 0], zs_r.at[e, 0], (md, up)),
            remote(ZU.at[e, 3], RU.at[e, 5], zs_s.at[e, 1], zs_r.at[e, 1], (right, up)),
            remote(ZU.at[e, 4], RU.at[e, 6], zs_s.at[e, 2], zs_r.at[e, 2], (left, up)),
            remote(ZD.at[e], RD.at[e, 0:5], zs_s.at[e, 3], zs_r.at[e, 3], (md, dn)),
            remote(ZD.at[e, 4], RD.at[e, 5], zs_s.at[e, 4], zs_r.at[e, 4], (right, dn)),
            remote(ZD.at[e, 3], RD.at[e, 6], zs_s.at[e, 5], zs_r.at[e, 5], (left, dn)),
        ]
        for c in out:
            c.start()
        return out

    def edges(e, sends):
        for c in sends[2:]:
            c.wait_recv()
        low = sub < NT
        is_open = W[...] == 1
        for k in range(5):
            for vertical, pop in ((0, UP[k]), (1, DOWN[k])):
                src = RD if vertical else RU
                cx = VELOCITIES[pop][0]
                tile = src[e, k]
                if cx == 1:
                    tile = pltpu.roll(jnp.where(low, tile, src[e, 5]), NT, 0)
                elif cx == -1:
                    tile = pltpu.roll(jnp.where(low, src[e, 6], tile), NT, 0)
                if vertical:
                    tile = jnp.where(th == 3, WEIGHTS[pop] * INLET_DENSITY, tile)
                    row = 40
                else:
                    solid_wire = jnp.concatenate([B[k, r, 0:1, :] for r in range(8)], axis=0)
                    wall = jnp.where(is_open, WEIGHTS[pop] * OUTLET_DENSITY, solid_wire)
                    tile = jnp.where(th == 0, wall, tile)
                    row = 7
                for x in range(2):
                    for t in range(NT):
                        r = x * NT + t
                        R[e, SLOT[pop], x + 1 - cx, t, row:row + 1, :] = tile[r:r + 1, :]
        for c in sends[:2]:
            c.wait_recv()

    for t in range(NT):
        loads[5 + t].wait()

    def first(x, t, z):
        rows = pl.ds(pl.multiple_of(z * 8, 8), 8)
        put(0, x, t, z, collide([F[i, x, t, rows, :] for i in range(19)], solid_at(x, t, z)))

    chunks(first)
    sent0 = exchange(0)

    def inverse(n, _):
        s, zc = n // 16, lax.rem(n, 16)
        d = jnp.full((8, LANES), diff[s], jnp.float32)
        h = 0.5 * lax.rsqrt(d)
        theta = 2.0 * jnp.log1p(h + h * h / (1.0 + jnp.sqrt(1.0 + h * h)))
        i = (sub + zc * 8).astype(jnp.float32)
        j = lane.astype(jnp.float32)
        gap = jnp.abs(i - j)
        total = i + j + 1.0
        full = 2.0 * LANES
        top = jnp.exp(-theta * gap) + jnp.exp(-theta * (full - gap))
        top = top + (jnp.exp(-theta * total) + jnp.exp(-theta * (full - total)))
        g = top / (jnp.sqrt(4.0 * d + 1.0) * (1.0 - jnp.exp(-theta * full)))
        G[s, pl.ds(pl.multiple_of(zc * 8, 8), 8), :] = g
        return 0

    lax.fori_loop(0, 64, inverse, 0)

    edges(0, sent0)

    def second(x, t, z):
        put(1, x, t, z, collide(pull(0, x, t, z), solid_at(x, t, z)))

    chunks(second)
    sent1 = exchange(1)
    edges(1, sent1)

    def third(x, t, z):
        f = pull(1, x, t, z)
        rows = pl.ds(pl.multiple_of(z * 8, 8), 8)
        for i in range(19):
            F[i, x, t, rows, :] = f[i]
        _, ux, uy, uz = moments(f)
        fluid = 1.0 - S[x, t, rows, :]
        V[0, x, t, rows, :] = ux * fluid
        V[1, x, t, rows, :] = uy * fluid
        V[2, x, t, rows, :] = uz * fluid

    chunks(third)
    speeds = [
        remote(V.at[:, :, p], Vall.at[:, :, my_rows, :], vs_s.at[k], vs_r.at[k], (md, p))
        for k, p in enumerate(peers)
    ]
    for c in speeds:
        c.start()
    stores = []
    for t in range(NT):
        stores.append(pltpu.make_async_copy(
            F.at[:, :, t], pops_out.at[:, :, :, t * LANES:(t + 1) * LANES], out_sem.at[t]))
    for c in stores:
        c.start()
    for a in range(3):
        for x in range(2):
            Vall[a, x, my_rows, :] = V[a, x, th]

    for c in solids:
        c.wait_recv()
    for c in speeds:
        c.wait_recv()

    def coefficients(n, _):
        x, zc = n // 16, lax.rem(n, 16)
        rows = pl.ds(pl.multiple_of(zc * 8, 8), 8)
        ux, uy, uz = [Vall[a, x, rows, :] for a in range(3)]
        C[0, x, rows, :] = (1.0 - 4.0 * LATERAL_DIFFUSION) - (jnp.abs(ux) + jnp.abs(uy) + jnp.abs(uz))
        C[1, x, rows, :] = LATERAL_DIFFUSION + jnp.maximum(ux, 0.0)
        C[2, x, rows, :] = LATERAL_DIFFUSION - jnp.minimum(ux, 0.0)
        C[3, x, rows, :] = LATERAL_DIFFUSION + jnp.maximum(uy, 0.0)
        C[4, x, rows, :] = LATERAL_DIFFUSION - jnp.minimum(uy, 0.0)
        C[5, x, rows, :] = jnp.maximum(uz, 0.0)
        C[6, x, rows, :] = -jnp.minimum(uz, 0.0)
        return 0

    lax.fori_loop(0, 32, coefficients, 0)

    def transport(step, s, sends):
        for x in range(2):
            Q[step, s, x + 1, 7:8, :] = Q[step, s, x + 1, 8:9, :]
            Q[step, s, x + 1, 136:137, :] = Q[step, s, x + 1, 135:136, :]
        for c in sends:
            c.wait_recv()
        west_in = YW[step, s]
        east_in = YE[step, s]

        def explicit(n, _):
            x, zc = n // 16, lax.rem(n, 16)
            rows = pl.ds(pl.multiple_of(zc * 8, 8), 8)
            held = pl.ds(pl.multiple_of(8 + zc * 8, 8), 8)
            c = Q[step, s, x + 1, held, :]
            below = Q[step, s, x + 1, pl.ds(7 + zc * 8, 8), :]
            above = Q[step, s, x + 1, pl.ds(9 + zc * 8, 8), :]
            south = jnp.where(lane == 0, pltpu.roll(west_in, lax.rem(LANES - n, LANES), 1), pltpu.roll(c, 1, 1))
            north = jnp.where(lane == LANES - 1, pltpu.roll(east_in, LANES - 1 - n, 1), pltpu.roll(c, LANES - 1, 1))
            value = c * (C[0, x, rows, :] - ret[s] * Sall[x, rows, :])
            value += Q[step, s, x, held, :] * C[1, x, rows, :]
            value += Q[step, s, x + 2, held, :] * C[2, x, rows, :]
            value += south * C[3, x, rows, :]
            value += north * C[4, x, rows, :]
            value += below * C[5, x, rows, :]
            value += above * C[6, x, rows, :]
            X[x, rows, :] = value
            return 0

        lax.fori_loop(0, 32, explicit, 0)
        g = G[s]
        g_hi = g.astype(jnp.bfloat16)
        g_lo = (g - g_hi.astype(jnp.float32)).astype(jnp.bfloat16)
        for x in range(2):
            v = X[x]
            v_hi = v.astype(jnp.bfloat16)
            v_lo = (v - v_hi.astype(jnp.float32)).astype(jnp.bfloat16)
            q = jnp.dot(g_lo, v_hi, preferred_element_type=jnp.float32)
            q += jnp.dot(g_hi, v_lo, preferred_element_type=jnp.float32)
            q += jnp.dot(g_hi, v_hi, preferred_element_type=jnp.float32)
            if step == 0:
                Q[1, s, x + 1, 8:136, :] = q
            else:
                X[2 + 2 * s + x] = q

    fine1 = []
    for s in range(4):
        transport(0, s, fine0[s])
        pack_columns(1, s, 1)
        sends = fine_sends(1, s)
        for c in sends:
            c.start()
        fine1.append(sends)
    for s in range(4):
        transport(1, s, fine1[s])
        c = pltpu.make_async_copy(X.at[2 + 2 * s:4 + 2 * s], fines_out.at[s], out_sem.at[NT + s])
        c.start()
        stores.append(c)

    for c in sent0 + sent1 + solids + speeds:
        c.wait_send()
    for group in fine0 + fine1:
        for c in group:
            c.wait_send()
    for c in stores:
        c.wait()


def on_device(populations, fibre_mask, wire_open, fines, diffusivity, retention):
    any_ = pl.BlockSpec(memory_space=pl.ANY)
    smem = pl.BlockSpec(memory_space=pltpu.SMEM)
    f32 = jnp.float32
    dma = pltpu.SemaphoreType.DMA
    return pl.pallas_call(
        kernel,
        out_shape=(
            jax.ShapeDtypeStruct(populations.shape, f32),
            jax.ShapeDtypeStruct(fines.shape, f32),
        ),
        in_specs=[any_, any_, pl.BlockSpec(memory_space=pltpu.VMEM), any_, smem, smem],
        out_specs=(any_, any_),
        scratch_shapes=[
            pltpu.VMEM((19, 2, NT, 32, LANES), f32),
            pltpu.VMEM((2, 19, 4, NT, 48, LANES), f32),
            pltpu.VMEM((2, NT, 32, LANES), jnp.int32),
            pltpu.VMEM((2, NT, 32, LANES), f32),
            pltpu.VMEM((2, 128, LANES), f32),
            pltpu.VMEM((3, 2, NT, 32, LANES), f32),
            pltpu.VMEM((3, 2, 128, LANES), f32),
            pltpu.VMEM((5, 8, 8, LANES), f32),
            pltpu.VMEM((2, 5, 8, LANES), f32),
            pltpu.VMEM((2, 5, 8, LANES), f32),
            pltpu.VMEM((2, 7, 8, LANES), f32),
            pltpu.VMEM((2, 7, 8, LANES), f32),
            pltpu.VMEM((8, LANES), jnp.int32),
            pltpu.VMEM((2, 4, 4, 144, LANES), f32),
            pltpu.VMEM((7, 2, 128, LANES), f32),
            pltpu.VMEM((10, 128, LANES), f32),
            pltpu.VMEM((4, 128, LANES), f32),
            pltpu.VMEM((2, 4, 2, 8, LANES), f32),
            pltpu.VMEM((2, 4, 8, LANES), f32),
            pltpu.VMEM((2, 4, 8, LANES), f32),
            dma((9,)), dma((8,)),
            dma((2, 2)), dma((2, 2)),
            dma((2, 6)), dma((2, 6)),
            dma((3,)), dma((3,)),
            dma((3,)), dma((3,)),
            dma((2, 4, 2)), dma((2, 4, 2)),
            dma((2, 4, 2)), dma((2, 4, 2)),
        ],
        compiler_params=pltpu.CompilerParams(
            collective_id=0, has_side_effects=True, vmem_limit_bytes=56 * 1024 * 1024),
        name="drainage",
    )(populations, fibre_mask, wire_open, fines, diffusivity, retention)


def solution(mesh):
    return jax.shard_map(
        on_device,
        mesh=mesh,
        in_specs=(
            P(None, "md", "th", None), P("md", "th", None), P("md", None),
            P(None, "md", None, "th"), P(), P(),
        ),
        out_specs=(P(None, "md", "th", None), P(None, "md", None, "th")),
        check_vma=False,
    )
```

profile of v0, /device:TPU:32, one launch (start us, length us, event | category | flops | bytes accessed | tf_op | source)
XLA Modules:
  0.0 116.6 jit_solution(15606720746376729615)
XLA Ops:
  0.6 111.6 %drainage.1 = (f32[19,2,32,512]{3,2,1,0:T(8,128)}, f32[4,2,128,128]{3,2,1,0:T(8,128)}) custom-call(f32[19,2,32,512]{3,2,1,0:T(8,128)} %pops.1, s32[2,32,512]{2,1,0:T(8,128)} %mask.1, s32[2,512]{1,0:T(2,128)} %wire.1, f32[4,2,128,128]{3,2,1,0:T(8,128)} %fines.1, f32[4]{0:T(128)} %diff.1, f32[4]{0:T(128)} %ret.1), custom_call_target="tpu_custom_call" | custom-call | tf_op jit(solution)/shard_map/drainage/pallas_call | solution.py:401
  112.2 0.0 copy-start
  112.3 3.6 %copy.10 = f32[19,2,32,512]{3,2,1,0:T(8,128)} copy(f32[19,2,32,512]{3,2,1,0:T(8,128)} %get-tuple-element.4) | data formatting | bytes 4980736
  115.8 0.0 copy-done
  115.8 0.8 copy.11
Async XLA Ops:
  112.2 3.6 %copy-start = (f32[4,2,128,128]{3,2,1,0:T(8,128)S(1)}, f32[4,2,128,128]{3,2,1,0:T(8,128)}, u32[]{:S(2)}) copy-start(f32[4,2,128,128]{3,2,1,0:T(8,128)} %get-tuple-element.5) | copy-start | bytes 1572868
where the time goes:
time: 117 us
  Pallas kernels  112 us (96%)
  local copies, waits for them, and re-layouts  4.38 us (4%)
    pallas_call x1, Pallas kernels, on_device(): pl.pallas_call(kernel, out_shape=(jax.ShapeDtypeStruct(populations.shape,...  112 us
    unnamed x4, local copies, waits for them, and re-layouts  4.38 us

commit v1 on v0

v1 whole, which is shorter than its diff:
```python
import functools

import jax
import jax.numpy as jnp
from jax import lax
from jax.experimental import pallas as pl
from jax.experimental.pallas import tpu as pltpu
from jax.sharding import PartitionSpec as P

VELOCITIES = [
    (0, 0, 0), (1, 0, 0), (-1, 0, 0), (0, 1, 0), (0, -1, 0), (0, 0, 1), (0, 0, -1),
    (1, 1, 0), (-1, -1, 0), (1, -1, 0), (-1, 1, 0), (1, 0, 1), (-1, 0, -1), (1, 0, -1),
    (-1, 0, 1), (0, 1, 1), (0, -1, -1), (0, 1, -1), (0, -1, 1),
]
WEIGHTS = [1.0 / 3.0] + [1.0 / 18.0] * 6 + [1.0 / 36.0] * 12
OPPOSITE = [0, 2, 1, 4, 3, 6, 5, 8, 7, 10, 9, 12, 11, 14, 13, 16, 15, 18, 17]
RELAXATION = 1.6
INLET_DENSITY = 1.03
OUTLET_DENSITY = 0.97
LATERAL_DIFFUSION = 0.1

PLUS = [1, 7, 9, 11, 13]
MINUS = [2, 8, 10, 12, 14]
ZERO = [0, 3, 4, 5, 6, 15, 16, 17, 18]
SLOT = {i: k for k, i in enumerate(PLUS + MINUS + ZERO)}
UP = [5, 15, 18, 11, 14]
DOWN = [6, 16, 17, 12, 13]

MESH = pl.DeviceIdType.MESH
LANES = 128
NT = 4
TOP = 8


def total(items):
    items = list(items)
    while len(items) > 1:
        items = [a + b for a, b in zip(items[::2], items[1::2])] + (
            [items[-1]] if len(items) % 2 else []
        )
    return items[0]


PAIRS = list(range(1, 19, 2))


def signed(terms):
    plus = [v for c, v in terms if c > 0]
    minus = [v for c, v in terms if c < 0]
    return total(plus) - total(minus) if minus else total(plus)


def pair_moments(f):
    even = {i: f[i] + f[i + 1] for i in PAIRS}
    odd = {i: f[i] - f[i + 1] for i in PAIRS}
    mass = total([f[0]] + [even[i] for i in PAIRS])
    flux = [
        signed([(VELOCITIES[i][a], odd[i]) for i in PAIRS if VELOCITIES[i][a]]) for a in range(3)
    ]
    return even, odd, mass, flux


def collide(f, solid):
    even, odd, mass, flux = pair_moments(f)
    scale = (4.5 ** 0.5) / mass
    px, py, pz = [v * scale for v in flux]
    base = 1.0 - (1.0 / 3.0) * (px * px + py * py + pz * pz)
    keep = 1.0 - RELAXATION
    k_even = jnp.where(solid, 0.5, 0.5 * keep)
    k_odd = jnp.where(solid, -0.5, 0.5 * keep)
    m_diag = jnp.where(solid, 0.0, (RELAXATION * WEIGHTS[7]) * mass)
    m_axis = m_diag + m_diag
    odd_diag, odd_axis = (2.0 ** 0.5) * m_diag, (2.0 ** 0.5) * m_axis
    out = [None] * 19
    out[0] = jnp.where(solid, 1.0, keep) * f[0] + (WEIGHTS[0] / WEIGHTS[7]) * (m_diag * base)
    for i in PAIRS:
        p = signed([(c, v) for c, v in zip(VELOCITIES[i], (px, py, pz)) if c])
        axis = i < 7
        a = k_even * even[i] + (m_axis if axis else m_diag) * (base + p * p)
        b = k_odd * odd[i] + (odd_axis if axis else odd_diag) * p
        out[i] = a + b
        out[i + 1] = a - b
    return out


DIRECT = 3


def kernel(
    pops, mask, wire_hbm, fines, diff_hbm, ret_hbm, pops_out, fines_out,
    wire, diff, ret, F, R0, R1, M, S, Sall, V, Vall, B, ZU, ZD, RU, RD, W, Q0, Q1, C, X, G, GB, YP, YW, YE, RB, QB,
    in_sem, xs_s, xs_r, zs_s, zs_r, ss_s, ss_r, vs_s, vs_r, q_s, q_r, y_s, y_r,
    rb_r, fw_s, qb_r, qf_s,
):
    md = lax.axis_index("md")
    th = lax.axis_index("th")
    nmd = lax.axis_size("md")
    right, left = lax.rem(md + 1, nmd), lax.rem(md + nmd - 1, nmd)
    up, dn = lax.rem(th + 1, 4), lax.rem(th + 3, 4)
    peers = [lax.rem(th + d, 4) for d in (1, 2, 3)]
    R = (R0, R1)
    Q = (Q0, Q1)
    first = lax.rem(md, 16) == 0
    last = lax.rem(md, 16) == 15
    corner = first | last
    opposite = jnp.where(first, lax.rem(md + 15, nmd), lax.rem(md + nmd - 15, nmd))
    ahead, behind = lax.rem(md + 16, nmd), lax.rem(md + nmd - 16, nmd)

    loads = [
        pltpu.make_async_copy(fines, Q0.at[:, 1:3, 8:136, :], in_sem.at[0]),
    ]
    for t in range(NT):
        loads.append(pltpu.make_async_copy(
            mask.at[:, :, t * LANES:(t + 1) * LANES], M.at[:, t], in_sem.at[1 + t]))
    for t in range(NT):
        loads.append(pltpu.make_async_copy(
            pops.at[:, :, :, t * LANES:(t + 1) * LANES], F.at[:, :, t], in_sem.at[5 + t]))
    small = [
        pltpu.make_async_copy(a, b, in_sem.at[9 + k])
        for k, (a, b) in enumerate(((wire_hbm, wire), (diff_hbm, diff), (ret_hbm, ret)))
    ]
    for c in loads + small:
        c.start()

    barrier = pltpu.get_barrier_semaphore()
    friends = [(right, th), (left, th)] + [(md, p) for p in peers]
    friends += [(m, t) for m in (right, left) for t in (up, dn)]
    for d in friends:
        pl.semaphore_signal(barrier, inc=1, device_id=d, device_id_type=MESH)

    @pl.when(corner)
    def _():
        for m in (opposite, ahead, behind):
            pl.semaphore_signal(barrier, inc=1, device_id=(m, th), device_id_type=MESH)

    lane = lax.broadcasted_iota(jnp.int32, (8, LANES), 1)
    sub = lax.broadcasted_iota(jnp.int32, (8, LANES), 0)

    def remote(src, dst, s, r, dev):
        return pltpu.make_async_remote_copy(
            src_ref=src, dst_ref=dst, send_sem=s, recv_sem=r, device_id=dev, device_id_type=MESH)

    def rows8(z):
        return pl.ds(pl.multiple_of(z * 8, 8), 8)

    for c in small:
        c.wait()
    for x in range(2):
        for t in range(NT):
            W[x * NT + t:x * NT + t + 1, :] = wire[x:x + 1, t * LANES:(t + 1) * LANES]

    def pack_columns(step, s):
        east = west = jnp.zeros((8, LANES), jnp.float32)
        for x in range(2):
            for zc in range(16):
                k = x * 16 + zc
                c = Q[step][s, x + 1, 8 + zc * 8:16 + zc * 8, :]
                east = jnp.where(lane == k, pltpu.roll(c, k + 1, 1), east)
                west = jnp.where(lane == k, pltpu.roll(c, k, 1) if k else c, west)
        YP[step, s, 0] = east
        YP[step, s, 1] = west

    def fine_copies(step, s):
        q = Q[step]
        return [
            remote(q.at[s, 2, 8:136, :], q.at[s, 0, 8:136, :], q_s.at[step, s, 0], q_r.at[step, s, 0], (right, th)),
            remote(q.at[s, 1, 8:136, :], q.at[s, 3, 8:136, :], q_s.at[step, s, 1], q_r.at[step, s, 1], (left, th)),
            remote(YP.at[step, s, 0], YW.at[step, s], y_s.at[step, s, 0], y_r.at[step, s, 0], (md, up)),
            remote(YP.at[step, s, 1], YE.at[step, s], y_s.at[step, s, 1], y_r.at[step, s, 1], (md, dn)),
        ]

    def start_fines(step, s):
        q = Q[step]
        k = s // 2
        relayed = lax.rem(s, 2) == 0
        copies = fine_copies(step, s)
        for side, edge, plane in ((0, last, 2), (1, first, 1)):
            via = relayed & edge

            @pl.when(via)
            def _():
                remote(q.at[s, plane, 8:136, :], QB.at[step, k], q_s.at[step, s, side], qb_r.at[step, k], (opposite, th)).start()

            @pl.when(jnp.logical_not(via))
            def _():
                copies[side].start()

        copies[2].start()
        copies[3].start()

    def fine_forwards(step, side, dev, plane):
        return [
            remote(QB.at[step, k], Q[step].at[2 * k, plane, 8:136, :], qf_s.at[step, k], q_r.at[step, 2 * k, side], (dev, th))
            for k in range(2)
        ]

    def forward_fines(step):
        arrivals = [
            remote(Q[step].at[2 * k, 1, 8:136, :], QB.at[step, k], q_s.at[step, 2 * k, 0], qb_r.at[step, k], (opposite, th))
            for k in range(2)
        ]

        @pl.when(first)
        def _():
            for a, c in zip(arrivals, fine_forwards(step, 0, ahead, 0)):
                a.wait_recv()
                c.start()

        @pl.when(last)
        def _():
            for a, c in zip(arrivals, fine_forwards(step, 1, behind, 3)):
                a.wait_recv()
                c.start()

    loads[0].wait()

    def pack_first(s, _):
        pack_columns(0, s)
        return 0

    lax.fori_loop(0, 4, pack_first, 0)
    for t in range(NT):
        loads[1 + t].wait()
    S[...] = M[...].astype(jnp.float32)

    @pl.when(corner)
    def _():
        pl.semaphore_wait(barrier, len(friends) + 3)

    @pl.when(jnp.logical_not(corner))
    def _():
        pl.semaphore_wait(barrier, len(friends))

    def send_first(s, _):
        start_fines(0, s)
        return 0

    lax.fori_loop(0, 4, send_first, 0)
    my_rows = pl.ds(pl.multiple_of(th * 32, 32), 32)
    solids = [
        remote(S.at[:, p], Sall.at[:, my_rows, :], ss_s.at[k], ss_r.at[k], (md, p))
        for k, p in enumerate(peers)
    ]
    for c in solids:
        c.start()
    for x in range(2):
        Sall[x, my_rows, :] = S[x, th]

    def put(e, x, t, z, out):
        rows = pl.ds(pl.multiple_of(8 + z * 8, 8), 8)
        r = R[e]
        for i in range(19):
            cy = VELOCITIES[i][1]
            k = SLOT[i]
            if cy == 0:
                r[k, x + 1, t, rows, :] = out[i]
            elif cy == 1:
                v = pltpu.roll(out[i], 1, 1)
                r[k, x + 1, t, rows, 1:LANES] = v[:, 1:LANES]
                r[k, x + 1, lax.rem(t + 1, NT), rows, 0:1] = v[:, 0:1]
            else:
                v = pltpu.roll(out[i], LANES - 1, 1)
                r[k, x + 1, t, rows, 0:LANES - 1] = v[:, 0:LANES - 1]
                r[k, x + 1, lax.rem(t + 3, NT), rows, LANES - 1:LANES] = v[:, LANES - 1:LANES]
        B[0, x * NT + t] = out[16]
        B[1, x * NT + t] = out[17]

    def solid_at(x, t, z):
        return S[x, t, rows8(z), :] > 0

    def chunks(body):
        def step(n, _):
            z = 3 - n // NT
            t = lax.rem(n, NT)
            for x in range(2):
                body(x, t, z)
            return 0
        lax.fori_loop(0, 16, step, 0)

    def pull(e, x, t, z):
        f = []
        for i in range(19):
            cx, _, cz = VELOCITIES[i]
            f.append(R[e][SLOT[i], x + 1 - cx, t, pl.ds(8 + z * 8 - cz, 8), :])
        return f

    def forwards(e, side, dev, plane):
        return [
            remote(RB.at[e, k], R[e].at[5 * side + DIRECT + k, plane, :, 8:40, :], fw_s.at[e, k], xs_r.at[e, side, 1 + k], (dev, th))
            for k in range(2)
        ]

    def exchange(e):
        r = R[e]
        out = []
        for side, edge, dev, src, dst in ((0, last, right, 2, 0), (1, first, left, 1, 3)):
            pieces, via = [], []
            for k in range(2):
                slot = 5 * side + DIRECT + k
                pieces.append(remote(r.at[slot, src, :, 8:40, :], r.at[slot, dst, :, 8:40, :], xs_s.at[e, side, 1 + k], xs_r.at[e, side, 1 + k], (dev, th)))
                via.append(remote(r.at[slot, src, :, 8:40, :], RB.at[e, k], xs_s.at[e, side, 1 + k], rb_r.at[e, k], (opposite, th)))

            @pl.when(edge)
            def _():
                for c in via:
                    c.start()

            @pl.when(jnp.logical_not(edge))
            def _():
                for c in pieces:
                    c.start()

            straight = slice(5 * side, 5 * side + DIRECT)
            c = remote(r.at[straight, src, :, 8:40, :], r.at[straight, dst, :, 8:40, :], xs_s.at[e, side, 0], xs_r.at[e, side, 0], (dev, th))
            c.start()
            out += [c] + pieces
        for k in range(5):
            for x in range(2):
                for t in range(NT):
                    n = x * NT + t
                    ZU[e, k, n:n + 1, :] = r[SLOT[UP[k]], x + 1, t, 39:40, :]
                    ZD[e, k, n:n + 1, :] = r[SLOT[DOWN[k]], x + 1, t, 8:9, :]
        rims = [
            remote(ZU.at[e], RU.at[e, 0:5], zs_s.at[e, 0], zs_r.at[e, 0], (md, up)),
            remote(ZU.at[e, 3], RU.at[e, 5], zs_s.at[e, 1], zs_r.at[e, 1], (right, up)),
            remote(ZU.at[e, 4], RU.at[e, 6], zs_s.at[e, 2], zs_r.at[e, 2], (left, up)),
            remote(ZD.at[e], RD.at[e, 0:5], zs_s.at[e, 3], zs_r.at[e, 3], (md, dn)),
            remote(ZD.at[e, 4], RD.at[e, 5], zs_s.at[e, 4], zs_r.at[e, 4], (right, dn)),
            remote(ZD.at[e, 3], RD.at[e, 6], zs_s.at[e, 5], zs_r.at[e, 5], (left, dn)),
        ]
        for c in rims:
            c.start()

        @pl.when(first)
        def _():
            for k, c in enumerate(forwards(e, 0, ahead, 0)):
                remote(r.at[8 + k, 1, :, 8:40, :], RB.at[e, k], xs_s.at[e, 1, 1 + k], rb_r.at[e, k], (opposite, th)).wait_recv()
                c.start()

        @pl.when(last)
        def _():
            for k, c in enumerate(forwards(e, 1, behind, 3)):
                remote(r.at[3 + k, 2, :, 8:40, :], RB.at[e, k], xs_s.at[e, 0, 1 + k], rb_r.at[e, k], (opposite, th)).wait_recv()
                c.start()

        return out, rims

    def edges(e, sends):
        bulk, rims = sends
        for c in rims:
            c.wait_recv()
        low = sub < NT
        is_open = W[...] == 1
        for k in range(5):
            for vertical, pop in ((0, UP[k]), (1, DOWN[k])):
                src = RD if vertical else RU
                cx = VELOCITIES[pop][0]
                tile = src[e, k]
                if cx == 1:
                    tile = pltpu.roll(jnp.where(low, tile, src[e, 5]), NT, 0)
                elif cx == -1:
                    tile = pltpu.roll(jnp.where(low, src[e, 6], tile), NT, 0)
                if vertical:
                    tile = jnp.where(th == 3, WEIGHTS[pop] * INLET_DENSITY, tile)
                    row = 40
                else:
                    if VELOCITIES[pop][1] == 0:
                        wall = ZD[e, k]
                    else:
                        wall = jnp.concatenate([B[k - 1, n, 0:1, :] for n in range(8)], axis=0)
                    wall = jnp.where(is_open, WEIGHTS[pop] * OUTLET_DENSITY, wall)
                    tile = jnp.where(th == 0, wall, tile)
                    row = 7
                for x in range(2):
                    for t in range(NT):
                        n = x * NT + t
                        R[e][SLOT[pop], x + 1 - cx, t, row:row + 1, :] = tile[n:n + 1, :]
        for c in bulk:
            c.wait_recv()

    for t in range(NT):
        loads[5 + t].wait()

    def flow_first(x, t, z):
        put(0, x, t, z, collide([F[i, x, t, rows8(z), :] for i in range(19)], solid_at(x, t, z)))

    chunks(flow_first)
    sent0 = exchange(0)
    forward_fines(0)

    def inverse(s, _):
        d = jnp.full((8, LANES), diff[s], jnp.float32)
        h = 0.5 * lax.rsqrt(d)
        theta = -2.0 * jnp.log1p(h + h * h / (1.0 + jnp.sqrt(1.0 + h * h)))
        j = lane.astype(jnp.float32)
        full = 2.0 * LANES
        norm = 1.0 / (jnp.sqrt(4.0 * d + 1.0) * (1.0 - jnp.exp(theta * full)))
        for zc in range(16):
            i = (sub + zc * 8).astype(jnp.float32)
            gap = jnp.abs(i - j)
            away = i + j + 1.0
            g = jnp.exp(theta * gap) + jnp.exp(theta * (full - gap))
            g = g + (jnp.exp(theta * away) + jnp.exp(theta * (full - away)))
            G[zc * 8:zc * 8 + 8, :] = g * norm
        g = G[...]
        hi = g.astype(jnp.bfloat16)
        GB[s, :, 0:LANES] = hi
        GB[s, :, LANES:2 * LANES] = (g - hi.astype(jnp.float32)).astype(jnp.bfloat16)
        return 0

    lax.fori_loop(0, 4, inverse, 0)

    edges(0, sent0)

    def flow_second(x, t, z):
        put(1, x, t, z, collide(pull(0, x, t, z), solid_at(x, t, z)))

    chunks(flow_second)
    sent1 = exchange(1)
    edges(1, sent1)

    def flow_last(x, t, z):
        f = pull(1, x, t, z)
        rows = rows8(z)
        for i in range(19):
            pops_out[i, x, rows, pl.ds(pl.multiple_of(t * LANES, LANES), LANES)] = f[i]
        _, _, mass, flux = pair_moments(f)
        fluid = (1.0 - S[x, t, rows, :]) / mass
        for a in range(3):
            V[a, x, t, rows, :] = flux[a] * fluid

    chunks(flow_last)
    speeds = [
        remote(V.at[:, :, p], Vall.at[:, :, my_rows, :], vs_s.at[k], vs_r.at[k], (md, p))
        for k, p in enumerate(peers)
    ]
    for c in speeds:
        c.start()
    for a in range(3):
        for x in range(2):
            Vall[a, x, my_rows, :] = V[a, x, th]

    for c in solids:
        c.wait_recv()
    for c in speeds:
        c.wait_recv()

    def coefficients(n, _):
        for x in range(2):
            for m in range(4):
                rows = rows8(n * 4 + m)
                ux, uy, uz = [Vall[a, x, rows, :] for a in range(3)]
                C[0, x, rows, :] = (1.0 - 4.0 * LATERAL_DIFFUSION) - (jnp.abs(ux) + jnp.abs(uy) + jnp.abs(uz))
                C[1, x, rows, :] = LATERAL_DIFFUSION + jnp.maximum(ux, 0.0)
                C[2, x, rows, :] = LATERAL_DIFFUSION - jnp.minimum(ux, 0.0)
                C[3, x, rows, :] = LATERAL_DIFFUSION + jnp.maximum(uy, 0.0)
                C[4, x, rows, :] = LATERAL_DIFFUSION - jnp.minimum(uy, 0.0)
                C[5, x, rows, :] = jnp.maximum(uz, 0.0)
                C[6, x, rows, :] = -jnp.minimum(uz, 0.0)
        return 0

    lax.fori_loop(0, 4, coefficients, 0)

    def transport(step, s):
        q = Q[step]
        for x in range(2):
            q[s, x + 1, 7:8, :] = q[s, x + 1, 8:9, :]
            q[s, x + 1, 136:137, :] = q[s, x + 1, 135:136, :]
        for c in fine_copies(step, s):
            c.wait_recv()
        west_in = YW[step, s]
        east_in = YE[step, s]
        kept = ret[s]
        for x in range(2):
            for zc in range(16):
                n = x * 16 + zc
                rows = slice(zc * 8, zc * 8 + 8)
                held = slice(zc * 8 + 8, zc * 8 + 16)
                c = q[s, x + 1, held, :]
                below = q[s, x + 1, zc * 8 + 7:zc * 8 + 15, :]
                above = q[s, x + 1, zc * 8 + 9:zc * 8 + 17, :]
                from_west = pltpu.roll(west_in, LANES - n, 1) if n else west_in
                from_east = pltpu.roll(east_in, LANES - 1 - n, 1)
                south = jnp.where(lane == 0, from_west, pltpu.roll(c, 1, 1))
                north = jnp.where(lane == LANES - 1, from_east, pltpu.roll(c, LANES - 1, 1))
                X[rows, x * LANES:(x + 1) * LANES] = total([
                    c * (C[0, x, rows, :] - kept * Sall[x, rows, :]),
                    q[s, x, held, :] * C[1, x, rows, :],
                    q[s, x + 2, held, :] * C[2, x, rows, :],
                    south * C[3, x, rows, :],
                    north * C[4, x, rows, :],
                    below * C[5, x, rows, :],
                    above * C[6, x, rows, :],
                ])
        v = X[...]
        v_hi = v.astype(jnp.bfloat16)
        v_lo = (v - v_hi.astype(jnp.float32)).astype(jnp.bfloat16)
        out = jnp.dot(GB[s], jnp.concatenate([v_hi, v_hi], axis=0), preferred_element_type=jnp.float32)
        out += jnp.dot(GB[s, :, 0:LANES], v_lo, preferred_element_type=jnp.float32)
        for x in range(2):
            part = out[:, x * LANES:(x + 1) * LANES]
            if step == 0:
                Q1[s, x + 1, 8:136, :] = part
            else:
                fines_out[s, x] = part

    def transport_first(s, _):
        transport(0, s)
        pack_columns(1, s)
        start_fines(1, s)
        return 0

    lax.fori_loop(0, 4, transport_first, 0)
    forward_fines(1)

    def transport_second(s, _):
        transport(1, s)
        return 0

    lax.fori_loop(0, 4, transport_second, 0)

    for c in sent0[0] + sent0[1] + sent1[0] + sent1[1] + solids + speeds:
        c.wait_send()
    for step in range(2):
        for s in range(4):
            for c in fine_copies(step, s):
                c.wait_send()

    @pl.when(corner)
    def _():
        for e in range(2):
            for c in forwards(e, 0, ahead, 0) + fine_forwards(e, 0, ahead, 0):
                c.wait_send()


def on_device(populations, fibre_mask, wire_open, fines, diffusivity, retention):
    any_ = pl.BlockSpec(memory_space=pl.ANY)
    vmem = pl.BlockSpec(memory_space=pltpu.VMEM)
    f32 = jnp.float32
    dma = pltpu.SemaphoreType.DMA
    populations_out, fines_out = pl.pallas_call(
        kernel,
        out_shape=(
            jax.ShapeDtypeStruct(populations.shape, f32),
            jax.ShapeDtypeStruct(fines.shape, f32),
        ),
        in_specs=[any_] * 6,
        out_specs=(vmem, vmem),
        scratch_shapes=[
            pltpu.VMEM(wire_open.shape, jnp.int32),
            pltpu.SMEM(diffusivity.shape, f32),
            pltpu.SMEM(retention.shape, f32),
            pltpu.VMEM((19, 2, NT, 32, LANES), f32),
            pltpu.VMEM((19, 4, NT, 48, LANES), f32),
            pltpu.VMEM((19, 4, NT, 48, LANES), f32),
            pltpu.VMEM((2, NT, 32, LANES), jnp.int32),
            pltpu.VMEM((2, NT, 32, LANES), f32),
            pltpu.VMEM((2, 128, LANES), f32),
            pltpu.VMEM((3, 2, NT, 32, LANES), f32),
            pltpu.VMEM((3, 2, 128, LANES), f32),
            pltpu.VMEM((2, 8, 8, LANES), f32),
            pltpu.VMEM((2, 5, 8, LANES), f32),
            pltpu.VMEM((2, 5, 8, LANES), f32),
            pltpu.VMEM((2, 7, 8, LANES), f32),
            pltpu.VMEM((2, 7, 8, LANES), f32),
            pltpu.VMEM((8, LANES), jnp.int32),
            pltpu.VMEM((4, 4, 144, LANES), f32),
            pltpu.VMEM((4, 4, 144, LANES), f32),
            pltpu.VMEM((7, 2, 128, LANES), f32),
            pltpu.VMEM((128, 2 * LANES), f32),
            pltpu.VMEM((128, LANES), f32),
            pltpu.VMEM((4, 128, 2 * LANES), jnp.bfloat16),
            pltpu.VMEM((2, 4, 2, 8, LANES), f32),
            pltpu.VMEM((2, 4, 8, LANES), f32),
            pltpu.VMEM((2, 4, 8, LANES), f32),
            pltpu.VMEM((2, 2, NT, 32, LANES), f32),
            pltpu.VMEM((2, 2, 128, LANES), f32),
            dma((12,)),
            dma((2, 2, 3)), dma((2, 2, 3)),
            dma((2, 6)), dma((2, 6)),
            dma((3,)), dma((3,)),
            dma((3,)), dma((3,)),
            dma((2, 4, 2)), dma((2, 4, 2)),
            dma((2, 4, 2)), dma((2, 4, 2)),
            dma((2, 2)), dma((2, 2)),
            dma((2, 2)), dma((2, 2)),
        ],
        compiler_params=pltpu.CompilerParams(
            collective_id=0, has_side_effects=True, vmem_limit_bytes=48 * 1024 * 1024),
        name="drainage",
    )(*[
        pltpu.with_memory_space_constraint(v, pltpu.HBM)
        for v in (populations, fibre_mask, wire_open, fines, diffusivity, retention)
    ])
    return populations_out, fines_out


def solution(mesh):
    return jax.shard_map(
        on_device,
        mesh=mesh,
        in_specs=(
            P(None, "md", "th", None), P("md", "th", None), P("md", None),
            P(None, "md", None, "th"), P(), P(),
        ),
        out_specs=(P(None, "md", "th", None), P(None, "md", None, "th")),
        check_vma=False,
    )
```

time: 117 us -> 75.7 us (0.65)
  the two profiles are of different devices: /device:TPU:32 before, /device:TPU:1 now
where the time goes in v1:
time: 75.7 us; the launch traced here: 75.6 us
  Pallas kernels  72.7 us (96%)
  local copies, waits for them, and re-layouts  2.24 us (3%)
    pallas_call x1, Pallas kernels, on_device(): pl.pallas_call(kernel, out_shape=(jax.ShapeDtypeStruct(populations.shape,...  72.7 us
    unnamed x2, local copies, waits for them, and re-layouts  2.24 us

profile of v1, /device:TPU:1, one launch (start us, length us, event | category | flops | bytes accessed | tf_op | source)
XLA Modules:
  0.0 75.6 jit_solution(15156859778778334030)
XLA Ops:
  0.6 72.7 %drainage.1 = (f32[19,2,32,512]{3,2,1,0:T(8,128)S(1)}, f32[4,2,128,128]{3,2,1,0:T(8,128)S(1)}) custom-call(f32[19,2,32,512]{3,2,1,0:T(8,128)} %pops.1, s32[2,32,512]{2,1,0:T(8,128)} %mask.1, s32[2,512]{1,0:T(2,128)} %wire_hbm.1, f32[4,2,128,128]{3,2,1,0:T(8,128)} %fines.1, f32[4]{0:T(128)} %diff_hbm.1, f32[4]{0:T(128)} %ret_hbm.1), custom_call_target="tpu_custom_call" | custom-call | tf_op jit(solution)/shard_map/drainage/pallas_call | solution.py:541
  73.3 1.5 %copy.10 = f32[19,2,32,512]{3,2,1,0:T(8,128)} copy(f32[19,2,32,512]{3,2,1,0:T(8,128)S(1)} %get-tuple-element.4) | data formatting | bytes 4980736
  74.8 0.8 %copy.11 = f32[4,2,128,128]{3,2,1,0:T(8,128)} copy(f32[4,2,128,128]{3,2,1,0:T(8,128)S(1)} %get-tuple-element.5) | data formatting | bytes 1048576

commit v2 on v1

--- a/solution.py
+++ b/solution.py
@@ -83,7 +83,9 @@
     return out
 
 
-DIRECT = 3
+QUARTERS = (3, 2, 1, 0)
+WAYS = {3: 0, 2: 1, 1: None, 0: None}
+RELAYED = 2
 
 
 def kernel(
@@ -100,23 +102,33 @@
     peers = [lax.rem(th + d, 4) for d in (1, 2, 3)]
     R = (R0, R1)
     Q = (Q0, Q1)
-    first = lax.rem(md, 16) == 0
-    last = lax.rem(md, 16) == 15
-    corner = first | last
-    opposite = jnp.where(first, lax.rem(md + 15, nmd), lax.rem(md + nmd - 15, nmd))
-    ahead, behind = lax.rem(md + 16, nmd), lax.rem(md + nmd - 16, nmd)
+    place = lax.rem(md, 16)
+    base = md - place
+    spot = {p: lax.rem(base + p, nmd) for p in (0, 3, 12, 15)}
+    ahead, behind = lax.rem(base + 16, nmd), lax.rem(base + nmd - 1, nmd)
+    by_way = ((spot[0], spot[3], spot[12]), (spot[15], spot[12], spot[3]))
+    source = (place == 15, place == 0)
+    is_relay = ((place == 0) | (place == 3) | (place == 12), (place == 15) | (place == 3) | (place == 12))
+    part = (
+        jnp.where(place == 0, 0, jnp.where(place == 3, 1, 2)),
+        jnp.where(place == 15, 0, jnp.where(place == 12, 1, 2)),
+    )
+    quarter_of = [jnp.where(p == 0, 3, jnp.where(p == 1, 2, 0)) for p in part]
+    species_of = [jnp.where(p == 0, 0, jnp.where(p == 1, 1, 0)) for p in part]
+    relays_flow = [is_relay[side] & ((part[side] == 0) | (part[side] == 1)) for side in range(2)]
+    relays_fines = [is_relay[side] & ((part[side] == 0) | (part[side] == 1)) for side in range(2)]
+    target = (ahead, behind)
+    came_from = (spot[15], spot[0])
 
     loads = [
         pltpu.make_async_copy(fines, Q0.at[:, 1:3, 8:136, :], in_sem.at[0]),
     ]
-    for t in range(NT):
+    loads.append(pltpu.make_async_copy(mask, M, in_sem.at[1]))
+    for z in QUARTERS:
         loads.append(pltpu.make_async_copy(
-            mask.at[:, :, t * LANES:(t + 1) * LANES], M.at[:, t], in_sem.at[1 + t]))
-    for t in range(NT):
-        loads.append(pltpu.make_async_copy(
-            pops.at[:, :, :, t * LANES:(t + 1) * LANES], F.at[:, :, t], in_sem.at[5 + t]))
+            pops.at[:, :, z * 8:z * 8 + 8, :], F.at[:, :, z * 8:z * 8 + 8, :], in_sem.at[2 + z]))
     small = [
-        pltpu.make_async_copy(a, b, in_sem.at[9 + k])
+        pltpu.make_async_copy(a, b, in_sem.at[6 + k])
         for k, (a, b) in enumerate(((wire_hbm, wire), (diff_hbm, diff), (ret_hbm, ret)))
     ]
     for c in loads + small:
@@ -128,10 +140,17 @@
     for d in friends:
         pl.semaphore_signal(barrier, inc=1, device_id=d, device_id_type=MESH)
 
-    @pl.when(corner)
-    def _():
-        for m in (opposite, ahead, behind):
-            pl.semaphore_signal(barrier, inc=1, device_id=(m, th), device_id_type=MESH)
+    more = {
+        0: [spot[15], spot[12], spot[3], ahead] + [lax.rem(base + nmd - 16 + p, nmd) for p in (0, 3, 12)],
+        15: [spot[0], spot[3], spot[12], behind] + [lax.rem(base + 16 + p, nmd) for p in (15, 12, 3)],
+        3: [spot[15], spot[0], ahead, behind],
+        12: [spot[15], spot[0], ahead, behind],
+    }
+    for p in more:
+        @pl.when(place == p)
+        def _(p=p):
+            for m in more[p]:
+                pl.semaphore_signal(barrier, inc=1, device_id=(m, th), device_id_type=MESH)
 
     lane = lax.broadcasted_iota(jnp.int32, (8, LANES), 1)
     sub = lax.broadcasted_iota(jnp.int32, (8, LANES), 0)
@@ -142,12 +161,6 @@
 
     def rows8(z):
         return pl.ds(pl.multiple_of(z * 8, 8), 8)
-
-    for c in small:
-        c.wait()
-    for x in range(2):
-        for t in range(NT):
-            W[x * NT + t:x * NT + t + 1, :] = wire[x:x + 1, t * LANES:(t + 1) * LANES]
 
     def pack_columns(step, s):
         east = west = jnp.zeros((8, LANES), jnp.float32)
@@ -169,85 +182,47 @@
             remote(YP.at[step, s, 1], YE.at[step, s], y_s.at[step, s, 1], y_r.at[step, s, 1], (md, dn)),
         ]
 
-    def start_fines(step, s):
+    def start_rows(step, s):
+        for c in fine_copies(step, s)[2:]:
+            c.start()
+
+    def start_planes(step, s):
         q = Q[step]
-        k = s // 2
-        relayed = lax.rem(s, 2) == 0
         copies = fine_copies(step, s)
-        for side, edge, plane in ((0, last, 2), (1, first, 1)):
-            via = relayed & edge
+        for side, plane in ((0, 2), (1, 1)):
+            a, b, c = [by_way[side][w] for w in (0, 1, 1)]
+            via = source[side] & (s < RELAYED)
+            dev = jnp.where(s == 0, a, jnp.where(s == 1, b, c))
 
             @pl.when(via)
             def _():
-                remote(q.at[s, plane, 8:136, :], QB.at[step, k], q_s.at[step, s, side], qb_r.at[step, k], (opposite, th)).start()
+                remote(q.at[s, plane, 8:136, :], QB.at[step, side], q_s.at[step, s, side], qb_r.at[step, side], (dev, th)).start()
 
             @pl.when(jnp.logical_not(via))
             def _():
                 copies[side].start()
 
-        copies[2].start()
-        copies[3].start()
-
-    def fine_forwards(step, side, dev, plane):
-        return [
-            remote(QB.at[step, k], Q[step].at[2 * k, plane, 8:136, :], qf_s.at[step, k], q_r.at[step, 2 * k, side], (dev, th))
-            for k in range(2)
-        ]
+    def fine_forward(step, side):
+        k = species_of[side]
+        return remote(QB.at[step, side], Q[step].at[k, 3 * side, 8:136, :], qf_s.at[step, side], q_r.at[step, k, side], (target[side], th))
 
     def forward_fines(step):
-        arrivals = [
-            remote(Q[step].at[2 * k, 1, 8:136, :], QB.at[step, k], q_s.at[step, 2 * k, 0], qb_r.at[step, k], (opposite, th))
-            for k in range(2)
-        ]
-
-        @pl.when(first)
-        def _():
-            for a, c in zip(arrivals, fine_forwards(step, 0, ahead, 0)):
-                a.wait_recv()
-                c.start()
-
-        @pl.when(last)
-        def _():
-            for a, c in zip(arrivals, fine_forwards(step, 1, behind, 3)):
-                a.wait_recv()
-                c.start()
-
-    loads[0].wait()
-
-    def pack_first(s, _):
-        pack_columns(0, s)
-        return 0
-
-    lax.fori_loop(0, 4, pack_first, 0)
+        for side in range(2):
+            @pl.when(relays_fines[side])
+            def _():
+                remote(Q[step].at[0, 1, 8:136, :], QB.at[step, side], qf_s.at[step, side], qb_r.at[step, side], (came_from[side], th)).wait_recv()
+                fine_forward(step, side).start()
+
+    loads[1].wait()
     for t in range(NT):
-        loads[1 + t].wait()
-    S[...] = M[...].astype(jnp.float32)
-
-    @pl.when(corner)
-    def _():
-        pl.semaphore_wait(barrier, len(friends) + 3)
-
-    @pl.when(jnp.logical_not(corner))
-    def _():
-        pl.semaphore_wait(barrier, len(friends))
-
-    def send_first(s, _):
-        start_fines(0, s)
-        return 0
-
-    lax.fori_loop(0, 4, send_first, 0)
+        S[:, t] = M[:, :, t * LANES:(t + 1) * LANES].astype(jnp.float32)
+
     my_rows = pl.ds(pl.multiple_of(th * 32, 32), 32)
-    solids = [
-        remote(S.at[:, p], Sall.at[:, my_rows, :], ss_s.at[k], ss_r.at[k], (md, p))
-        for k, p in enumerate(peers)
-    ]
-    for c in solids:
-        c.start()
     for x in range(2):
         Sall[x, my_rows, :] = S[x, th]
 
     def put(e, x, t, z, out):
-        rows = pl.ds(pl.multiple_of(8 + z * 8, 8), 8)
+        rows = slice(8 + z * 8, 16 + z * 8)
         r = R[e]
         for i in range(19):
             cy = VELOCITIES[i][1]
@@ -262,65 +237,40 @@
                 v = pltpu.roll(out[i], LANES - 1, 1)
                 r[k, x + 1, t, rows, 0:LANES - 1] = v[:, 0:LANES - 1]
                 r[k, x + 1, lax.rem(t + 3, NT), rows, LANES - 1:LANES] = v[:, LANES - 1:LANES]
-        B[0, x * NT + t] = out[16]
-        B[1, x * NT + t] = out[17]
+        if z == 0:
+            B[0, x * NT + t] = out[16]
+            B[1, x * NT + t] = out[17]
 
     def solid_at(x, t, z):
-        return S[x, t, rows8(z), :] > 0
-
-    def chunks(body):
-        def step(n, _):
-            z = 3 - n // NT
-            t = lax.rem(n, NT)
+        return S[x, t, z * 8:z * 8 + 8, :] > 0
+
+    def chunks(z, body):
+        def step(t, _):
             for x in range(2):
                 body(x, t, z)
             return 0
-        lax.fori_loop(0, 16, step, 0)
+        lax.fori_loop(0, NT, step, 0)
+
+    def tile(t):
+        return pl.ds(pl.multiple_of(t * LANES, LANES), LANES)
 
     def pull(e, x, t, z):
         f = []
         for i in range(19):
             cx, _, cz = VELOCITIES[i]
-            f.append(R[e][SLOT[i], x + 1 - cx, t, pl.ds(8 + z * 8 - cz, 8), :])
+            f.append(R[e][SLOT[i], x + 1 - cx, t, 8 + z * 8 - cz:16 + z * 8 - cz, :])
         return f
 
-    def forwards(e, side, dev, plane):
+    def quarter(e, side, z):
+        r = R[e]
+        rows = slice(8 + z * 8, 16 + z * 8)
+        slots = slice(5 * side, 5 * side + 5)
+        return remote(
+            r.at[slots, 2 - side, :, rows, :], r.at[slots, 3 * side, :, rows, :],
+            xs_s.at[e, side, z], xs_r.at[e, side, z], ((right, left)[side], th))
+
+    def rim_copies(e):
         return [
-            remote(RB.at[e, k], R[e].at[5 * side + DIRECT + k, plane, :, 8:40, :], fw_s.at[e, k], xs_r.at[e, side, 1 + k], (dev, th))
-            for k in range(2)
-        ]
-
-    def exchange(e):
-        r = R[e]
-        out = []
-        for side, edge, dev, src, dst in ((0, last, right, 2, 0), (1, first, left, 1, 3)):
-            pieces, via = [], []
-            for k in range(2):
-                slot = 5 * side + DIRECT + k
-                pieces.append(remote(r.at[slot, src, :, 8:40, :], r.at[slot, dst, :, 8:40, :], xs_s.at[e, side, 1 + k], xs_r.at[e, side, 1 + k], (dev, th)))
-                via.append(remote(r.at[slot, src, :, 8:40, :], RB.at[e, k], xs_s.at[e, side, 1 + k], rb_r.at[e, k], (opposite, th)))
-
-            @pl.when(edge)
-            def _():
-                for c in via:
-                    c.start()
-
-            @pl.when(jnp.logical_not(edge))
-            def _():
-                for c in pieces:
-                    c.start()
-
-            straight = slice(5 * side, 5 * side + DIRECT)
-            c = remote(r.at[straight, src, :, 8:40, :], r.at[straight, dst, :, 8:40, :], xs_s.at[e, side, 0], xs_r.at[e, side, 0], (dev, th))
-            c.start()
-            out += [c] + pieces
-        for k in range(5):
-            for x in range(2):
-                for t in range(NT):
-                    n = x * NT + t
-                    ZU[e, k, n:n + 1, :] = r[SLOT[UP[k]], x + 1, t, 39:40, :]
-                    ZD[e, k, n:n + 1, :] = r[SLOT[DOWN[k]], x + 1, t, 8:9, :]
-        rims = [
             remote(ZU.at[e], RU.at[e, 0:5], zs_s.at[e, 0], zs_r.at[e, 0], (md, up)),
             remote(ZU.at[e, 3], RU.at[e, 5], zs_s.at[e, 1], zs_r.at[e, 1], (right, up)),
             remote(ZU.at[e, 4], RU.at[e, 6], zs_s.at[e, 2], zs_r.at[e, 2], (left, up)),
@@ -328,65 +278,144 @@
             remote(ZD.at[e, 4], RD.at[e, 5], zs_s.at[e, 4], zs_r.at[e, 4], (right, dn)),
             remote(ZD.at[e, 3], RD.at[e, 6], zs_s.at[e, 5], zs_r.at[e, 5], (left, dn)),
         ]
-        for c in rims:
-            c.start()
-
-        @pl.when(first)
-        def _():
-            for k, c in enumerate(forwards(e, 0, ahead, 0)):
-                remote(r.at[8 + k, 1, :, 8:40, :], RB.at[e, k], xs_s.at[e, 1, 1 + k], rb_r.at[e, k], (opposite, th)).wait_recv()
+
+    def send(e, z):
+        r = R[e]
+        if z in (3, 0):
+            pack, list_, row = (ZU, UP, 39) if z == 3 else (ZD, DOWN, 8)
+            for k in range(5):
+                for x in range(2):
+                    for t in range(NT):
+                        n = x * NT + t
+                        pack[e, k, n:n + 1, :] = r[SLOT[list_[k]], x + 1, t, row:row + 1, :]
+            for c in rim_copies(e)[0 if z == 3 else 3:][:3]:
                 c.start()
-
-        @pl.when(last)
-        def _():
-            for k, c in enumerate(forwards(e, 1, behind, 3)):
-                remote(r.at[3 + k, 2, :, 8:40, :], RB.at[e, k], xs_s.at[e, 0, 1 + k], rb_r.at[e, k], (opposite, th)).wait_recv()
+        rows = slice(8 + z * 8, 16 + z * 8)
+        for side in range(2):
+            c = quarter(e, side, z)
+            if WAYS[z] is None:
                 c.start()
-
-        return out, rims
-
-    def edges(e, sends):
-        bulk, rims = sends
-        for c in rims:
+                continue
+
+            @pl.when(source[side])
+            def _():
+                slots = slice(5 * side, 5 * side + 5)
+                remote(r.at[slots, 2 - side, :, rows, :], RB.at[e, side], xs_s.at[e, side, z], rb_r.at[e, side], (by_way[side][WAYS[z]], th)).start()
+
+            @pl.when(jnp.logical_not(source[side]))
+            def _():
+                c.start()
+
+    def forward(e, side):
+        z = quarter_of[side]
+        rows = pl.ds(pl.multiple_of(8 + z * 8, 8), 8)
+        slots = slice(5 * side, 5 * side + 5)
+        return remote(RB.at[e, side], R[e].at[slots, 3 * side, :, rows, :], fw_s.at[e, side], xs_r.at[e, side, z], (target[side], th))
+
+    def relay(e):
+        for side in range(2):
+            @pl.when(relays_flow[side])
+            def _():
+                slots = slice(5 * side, 5 * side + 5)
+                remote(R[e].at[slots, 2 - side, :, 8:16, :], RB.at[e, side], fw_s.at[e, side], rb_r.at[e, side], (came_from[side], th)).wait_recv()
+                forward(e, side).start()
+
+    def rims(e, vertical):
+        for c in rim_copies(e)[3 * vertical:3 * vertical + 3]:
             c.wait_recv()
         low = sub < NT
         is_open = W[...] == 1
+        src = RD if vertical else RU
         for k in range(5):
-            for vertical, pop in ((0, UP[k]), (1, DOWN[k])):
-                src = RD if vertical else RU
-                cx = VELOCITIES[pop][0]
-                tile = src[e, k]
-                if cx == 1:
-                    tile = pltpu.roll(jnp.where(low, tile, src[e, 5]), NT, 0)
-                elif cx == -1:
-                    tile = pltpu.roll(jnp.where(low, src[e, 6], tile), NT, 0)
-                if vertical:
-                    tile = jnp.where(th == 3, WEIGHTS[pop] * INLET_DENSITY, tile)
-                    row = 40
+            pop = DOWN[k] if vertical else UP[k]
+            cx = VELOCITIES[pop][0]
+            rim = src[e, k]
+            if cx == 1:
+                rim = pltpu.roll(jnp.where(low, rim, src[e, 5]), NT, 0)
+            elif cx == -1:
+                rim = pltpu.roll(jnp.where(low, src[e, 6], rim), NT, 0)
+            if vertical:
+                rim = jnp.where(th == 3, WEIGHTS[pop] * INLET_DENSITY, rim)
+                row = 40
+            else:
+                if VELOCITIES[pop][1] == 0:
+                    wall = ZD[e, k]
                 else:
-                    if VELOCITIES[pop][1] == 0:
-                        wall = ZD[e, k]
-                    else:
-                        wall = jnp.concatenate([B[k - 1, n, 0:1, :] for n in range(8)], axis=0)
-                    wall = jnp.where(is_open, WEIGHTS[pop] * OUTLET_DENSITY, wall)
-                    tile = jnp.where(th == 0, wall, tile)
-                    row = 7
-                for x in range(2):
-                    for t in range(NT):
-                        n = x * NT + t
-                        R[e][SLOT[pop], x + 1 - cx, t, row:row + 1, :] = tile[n:n + 1, :]
-        for c in bulk:
-            c.wait_recv()
-
-    for t in range(NT):
-        loads[5 + t].wait()
+                    wall = jnp.concatenate([B[k - 1, n, 0:1, :] for n in range(8)], axis=0)
+                wall = jnp.where(is_open, WEIGHTS[pop] * OUTLET_DENSITY, wall)
+                rim = jnp.where(th == 0, wall, rim)
+                row = 7
+            for x in range(2):
+                for t in range(NT):
+                    n = x * NT + t
+                    R[e][SLOT[pop], x + 1 - cx, t, row:row + 1, :] = rim[n:n + 1, :]
+
+    def arrive(e, z):
+        if z == 3:
+            quarter(e, 0, 3).wait_recv()
+            quarter(e, 1, 3).wait_recv()
+            rims(e, 1)
+        if z > 0:
+            quarter(e, 0, z - 1).wait_recv()
+            quarter(e, 1, z - 1).wait_recv()
+        else:
+            rims(e, 0)
+
+    def await_friends():
+        @pl.when(source[0] | source[1])
+        def _():
+            pl.semaphore_wait(barrier, len(friends) + 7)
+
+        @pl.when((place == 3) | (place == 12))
+        def _():
+            pl.semaphore_wait(barrier, len(friends) + 4)
+
+        @pl.when(jnp.logical_not(is_relay[0] | is_relay[1]))
+        def _():
+            pl.semaphore_wait(barrier, len(friends))
 
     def flow_first(x, t, z):
-        put(0, x, t, z, collide([F[i, x, t, rows8(z), :] for i in range(19)], solid_at(x, t, z)))
-
-    chunks(flow_first)
-    sent0 = exchange(0)
+        rows = slice(z * 8, z * 8 + 8)
+        put(0, x, t, z, collide([F[i, x, rows, tile(t)] for i in range(19)], solid_at(x, t, z)))
+
+    solids = [
+        remote(S.at[:, p], Sall.at[:, my_rows, :], ss_s.at[k], ss_r.at[k], (md, p))
+        for k, p in enumerate(peers)
+    ]
+    def planes(s, _):
+        start_planes(0, s)
+        return 0
+
+    for z in QUARTERS:
+        loads[2 + QUARTERS.index(z)].wait()
+        chunks(z, flow_first)
+        if z == 3:
+            await_friends()
+        send(0, z)
+    loads[0].wait()
+    lax.fori_loop(0, 4, planes, 0)
+    relay(0)
     forward_fines(0)
+
+    def pack_first(s, _):
+        pack_columns(0, s)
+        return 0
+
+    lax.fori_loop(0, 4, pack_first, 0)
+
+    def send_rows(s, _):
+        start_rows(0, s)
+        return 0
+
+    lax.fori_loop(0, 4, send_rows, 0)
+    for c in solids:
+        c.start()
+    for c in small:
+        c.wait()
+    for x in range(2):
+        for t in range(NT):
+            W[x * NT + t:x * NT + t + 1, :] = wire[x:x + 1, t * LANES:(t + 1) * LANES]
+
 
     def inverse(s, _):
         d = jnp.full((8, LANES), diff[s], jnp.float32)
@@ -410,40 +439,47 @@
 
     lax.fori_loop(0, 4, inverse, 0)
 
-    edges(0, sent0)
-
     def flow_second(x, t, z):
         put(1, x, t, z, collide(pull(0, x, t, z), solid_at(x, t, z)))
 
-    chunks(flow_second)
-    sent1 = exchange(1)
-    edges(1, sent1)
+    for z in QUARTERS:
+        arrive(0, z)
+        chunks(z, flow_second)
+        send(1, z)
+
+    relay(1)
 
     def flow_last(x, t, z):
         f = pull(1, x, t, z)
-        rows = rows8(z)
+        rows = slice(z * 8, z * 8 + 8)
         for i in range(19):
-            pops_out[i, x, rows, pl.ds(pl.multiple_of(t * LANES, LANES), LANES)] = f[i]
+            pops_out[i, x, rows, tile(t)] = f[i]
         _, _, mass, flux = pair_moments(f)
         fluid = (1.0 - S[x, t, rows, :]) / mass
         for a in range(3):
             V[a, x, t, rows, :] = flux[a] * fluid
 
-    chunks(flow_last)
-    speeds = [
-        remote(V.at[:, :, p], Vall.at[:, :, my_rows, :], vs_s.at[k], vs_r.at[k], (md, p))
-        for k, p in enumerate(peers)
-    ]
-    for c in speeds:
-        c.start()
+    def speeds(z):
+        there = pl.ds(pl.multiple_of(th * 32 + z * 8, 8), 8)
+        return [
+            remote(V.at[:, :, p, z * 8:z * 8 + 8, :], Vall.at[:, :, there, :], vs_s.at[k, z], vs_r.at[k, z], (md, p))
+            for k, p in enumerate(peers)
+        ]
+
+    for z in QUARTERS:
+        arrive(1, z)
+        chunks(z, flow_last)
+        for c in speeds(z):
+            c.start()
     for a in range(3):
         for x in range(2):
             Vall[a, x, my_rows, :] = V[a, x, th]
 
     for c in solids:
         c.wait_recv()
-    for c in speeds:
-        c.wait_recv()
+    for z in QUARTERS:
+        for c in speeds(z):
+            c.wait_recv()
 
     def coefficients(n, _):
         for x in range(2):
@@ -507,7 +543,8 @@
     def transport_first(s, _):
         transport(0, s)
         pack_columns(1, s)
-        start_fines(1, s)
+        start_rows(1, s)
+        start_planes(1, s)
         return 0
 
     lax.fori_loop(0, 4, transport_first, 0)
@@ -519,18 +556,28 @@
 
     lax.fori_loop(0, 4, transport_second, 0)
 
-    for c in sent0[0] + sent0[1] + sent1[0] + sent1[1] + solids + speeds:
+    for c in solids:
         c.wait_send()
+    for z in QUARTERS:
+        for c in speeds(z):
+            c.wait_send()
+        for e in range(2):
+            for side in range(2):
+                quarter(e, side, z).wait_send()
     for step in range(2):
+        for c in rim_copies(step):
+            c.wait_send()
         for s in range(4):
             for c in fine_copies(step, s):
                 c.wait_send()
-
-    @pl.when(corner)
-    def _():
-        for e in range(2):
-            for c in forwards(e, 0, ahead, 0) + fine_forwards(e, 0, ahead, 0):
-                c.wait_send()
+        for side in range(2):
+            @pl.when(relays_flow[side])
+            def _():
+                forward(step, side).wait_send()
+
+            @pl.when(relays_fines[side])
+            def _():
+                fine_forward(step, side).wait_send()
 
 
 def on_device(populations, fibre_mask, wire_open, fines, diffusivity, retention):
@@ -550,10 +597,10 @@
             pltpu.VMEM(wire_open.shape, jnp.int32),
             pltpu.SMEM(diffusivity.shape, f32),
             pltpu.SMEM(retention.shape, f32),
-            pltpu.VMEM((19, 2, NT, 32, LANES), f32),
+            pltpu.VMEM(populations.shape, f32),
             pltpu.VMEM((19, 4, NT, 48, LANES), f32),
             pltpu.VMEM((19, 4, NT, 48, LANES), f32),
-            pltpu.VMEM((2, NT, 32, LANES), jnp.int32),
+            pltpu.VMEM(fibre_mask.shape, jnp.int32),
             pltpu.VMEM((2, NT, 32, LANES), f32),
             pltpu.VMEM((2, 128, LANES), f32),
             pltpu.VMEM((3, 2, NT, 32, LANES), f32),
@@ -573,13 +620,13 @@
             pltpu.VMEM((2, 4, 2, 8, LANES), f32),
             pltpu.VMEM((2, 4, 8, LANES), f32),
             pltpu.VMEM((2, 4, 8, LANES), f32),
-            pltpu.VMEM((2, 2, NT, 32, LANES), f32),
+            pltpu.VMEM((2, 2, 5, NT, 8, LANES), f32),
             pltpu.VMEM((2, 2, 128, LANES), f32),
-            dma((12,)),
-            dma((2, 2, 3)), dma((2, 2, 3)),
+            dma((9,)),
+            dma((2, 2, 4)), dma((2, 2, 4)),
             dma((2, 6)), dma((2, 6)),
             dma((3,)), dma((3,)),
-            dma((3,)), dma((3,)),
+            dma((3, 4)), dma((3, 4)),
             dma((2, 4, 2)), dma((2, 4, 2)),
             dma((2, 4, 2)), dma((2, 4, 2)),
             dma((2, 2)), dma((2, 2)),

time: 75.7 us -> 62.2 us (0.82)
  the two profiles are of different devices: /device:TPU:1 before, /device:TPU:32 now
where the time goes in v2:
time: 62.2 us; the launch traced here: 62.1 us
  Pallas kernels  59.2 us (95%)
  local copies, waits for them, and re-layouts  2.24 us (4%)
  between operations  0.64 us (1%)
    pallas_call x1, Pallas kernels, on_device(): pl.pallas_call(kernel, out_shape=(jax.ShapeDtypeStruct(populations.shape,...  59.2 us
    unnamed x2, local copies, waits for them, and re-layouts  2.24 us

profile of v2, /device:TPU:32, one launch (start us, length us, event | category | flops | bytes accessed | tf_op | source)
XLA Modules:
  0.0 62.1 jit_solution(17998611615094443121)
XLA Ops:
  0.6 59.2 %drainage.1 = (f32[19,2,32,512]{3,2,1,0:T(8,128)S(1)}, f32[4,2,128,128]{3,2,1,0:T(8,128)S(1)}) custom-call(f32[19,2,32,512]{3,2,1,0:T(8,128)} %pops.1, s32[2,32,512]{2,1,0:T(8,128)} %mask.1, s32[2,512]{1,0:T(2,128)} %wire_hbm.1, f32[4,2,128,128]{3,2,1,0:T(8,128)} %fines.1, f32[4]{0:T(128)} %diff_hbm.1, f32[4]{0:T(128)} %ret_hbm.1), custom_call_target="tpu_custom_call" | custom-call | tf_op jit(solution)/shard_map/drainage/pallas_call | solution.py:588
  59.8 1.5 %copy.10 = f32[19,2,32,512]{3,2,1,0:T(8,128)} copy(f32[19,2,32,512]{3,2,1,0:T(8,128)S(1)} %get-tuple-element.4) | data formatting | bytes 4980736
  61.3 0.8 %copy.11 = f32[4,2,128,128]{3,2,1,0:T(8,128)} copy(f32[4,2,128,128]{3,2,1,0:T(8,128)S(1)} %get-tuple-element.5) | data formatting | bytes 1048576

commit v3 on v2

--- a/solution.py
+++ b/solution.py
@@ -106,9 +106,9 @@
     base = md - place
     spot = {p: lax.rem(base + p, nmd) for p in (0, 3, 12, 15)}
     ahead, behind = lax.rem(base + 16, nmd), lax.rem(base + nmd - 1, nmd)
-    by_way = ((spot[0], spot[3], spot[12]), (spot[15], spot[12], spot[3]))
+    by_way = ((spot[0], spot[3]), (spot[15], spot[12]))
     source = (place == 15, place == 0)
-    is_relay = ((place == 0) | (place == 3) | (place == 12), (place == 15) | (place == 3) | (place == 12))
+    is_relay = ((place == 0) | (place == 3), (place == 15) | (place == 12))
     part = (
         jnp.where(place == 0, 0, jnp.where(place == 3, 1, 2)),
         jnp.where(place == 15, 0, jnp.where(place == 12, 1, 2)),
@@ -141,10 +141,10 @@
         pl.semaphore_signal(barrier, inc=1, device_id=d, device_id_type=MESH)
 
     more = {
-        0: [spot[15], spot[12], spot[3], ahead] + [lax.rem(base + nmd - 16 + p, nmd) for p in (0, 3, 12)],
-        15: [spot[0], spot[3], spot[12], behind] + [lax.rem(base + 16 + p, nmd) for p in (15, 12, 3)],
-        3: [spot[15], spot[0], ahead, behind],
-        12: [spot[15], spot[0], ahead, behind],
+        0: [spot[15], spot[12], ahead] + [lax.rem(base + nmd - 16 + p, nmd) for p in (0, 3)],
+        15: [spot[0], spot[3], behind] + [lax.rem(base + 16 + p, nmd) for p in (15, 12)],
+        3: [spot[15], ahead],
+        12: [spot[0], behind],
     }
     for p in more:
         @pl.when(place == p)
@@ -364,11 +364,11 @@
     def await_friends():
         @pl.when(source[0] | source[1])
         def _():
-            pl.semaphore_wait(barrier, len(friends) + 7)
+            pl.semaphore_wait(barrier, len(friends) + 5)
 
         @pl.when((place == 3) | (place == 12))
         def _():
-            pl.semaphore_wait(barrier, len(friends) + 4)
+            pl.semaphore_wait(barrier, len(friends) + 2)
 
         @pl.when(jnp.logical_not(is_relay[0] | is_relay[1]))
         def _():
@@ -474,6 +474,18 @@
     for a in range(3):
         for x in range(2):
             Vall[a, x, my_rows, :] = V[a, x, th]
+
+    for c in solids:
+        c.wait_send()
+    for e in range(2):
+        for c in rim_copies(e):
+            c.wait_send()
+        for z in QUARTERS:
+            for side in range(2):
+                quarter(e, side, z).wait_send()
+    for s in range(4):
+        for c in fine_copies(0, s):
+            c.wait_send()
 
     for c in solids:
         c.wait_recv()
@@ -542,9 +554,9 @@
 
     def transport_first(s, _):
         transport(0, s)
+        start_planes(1, s)
         pack_columns(1, s)
         start_rows(1, s)
-        start_planes(1, s)
         return 0
 
     lax.fori_loop(0, 4, transport_first, 0)
@@ -556,20 +568,13 @@
 
     lax.fori_loop(0, 4, transport_second, 0)
 
-    for c in solids:
-        c.wait_send()
+    for s in range(4):
+        for c in fine_copies(1, s):
+            c.wait_send()
     for z in QUARTERS:
         for c in speeds(z):
             c.wait_send()
-        for e in range(2):
-            for side in range(2):
-                quarter(e, side, z).wait_send()
     for step in range(2):
-        for c in rim_copies(step):
-            c.wait_send()
-        for s in range(4):
-            for c in fine_copies(step, s):
-                c.wait_send()
         for side in range(2):
             @pl.when(relays_flow[side])
             def _():
@@ -578,6 +583,35 @@
             @pl.when(relays_fines[side])
             def _():
                 fine_forward(step, side).wait_send()
+
+
+def put_out_kernel(a, b, a_out, b_out, sem):
+    copies = [
+        pltpu.make_async_copy(a.at[:, :, z * 8:z * 8 + 8, :], a_out.at[:, :, z * 8:z * 8 + 8, :], sem.at[z])
+        for z in range(4)
+    ]
+    copies.append(pltpu.make_async_copy(b, b_out, sem.at[4]))
+    for c in copies:
+        c.start()
+    for c in copies:
+        c.wait()
+
+
+def put_out(populations_out, fines_out):
+    vmem = pl.BlockSpec(memory_space=pltpu.VMEM)
+    any_ = pl.BlockSpec(memory_space=pltpu.HBM)
+    return pl.pallas_call(
+        put_out_kernel,
+        out_shape=(
+            jax.ShapeDtypeStruct(populations_out.shape, jnp.float32),
+            jax.ShapeDtypeStruct(fines_out.shape, jnp.float32),
+        ),
+        in_specs=[vmem, vmem],
+        out_specs=(any_, any_),
+        scratch_shapes=[pltpu.SemaphoreType.DMA((5,))],
+        compiler_params=pltpu.CompilerParams(vmem_limit_bytes=1024 * 1024),
+        name="put_out",
+    )(populations_out, fines_out)
 
 
 def on_device(populations, fibre_mask, wire_open, fines, diffusivity, retention):
@@ -639,7 +673,7 @@
         pltpu.with_memory_space_constraint(v, pltpu.HBM)
         for v in (populations, fibre_mask, wire_open, fines, diffusivity, retention)
     ])
-    return populations_out, fines_out
+    return put_out(populations_out, fines_out)
 
 
 def solution(mesh):

time: 62.2 us -> 61.2 us (0.984)
  local copies, waits for them, and re-layouts: 2.24 us -> 0 us
  Pallas kernels: 59.2 us -> 60.5 us
    unnamed x2 -> x0, local copies, waits for them, and re-layouts: 2.24 us -> none
    pallas_call x0 -> x1, Pallas kernels: none -> 1.66 us  [put_out(): pl.pallas_call(put_out_kernel, out_shape=(jax.ShapeDtypeStruct(population...]
where the time goes in v3:
time: 61.2 us
  Pallas kernels  60.5 us (99%)
  between operations  0.64 us (1%)
    pallas_call x1, Pallas kernels, on_device(): pl.pallas_call(kernel, out_shape=(jax.ShapeDtypeStruct(populations.shape,...  58.9 us
    pallas_call x1, Pallas kernels, put_out(): pl.pallas_call(put_out_kernel, out_shape=(jax.ShapeDtypeStruct(population...  1.66 us

profile of v3, /device:TPU:32, one launch (start us, length us, event | category | flops | bytes accessed | tf_op | source)
XLA Modules:
  0.0 61.2 jit_solution(16632902323345120416)
XLA Ops:
  0.6 58.9 %drainage.1 = (f32[19,2,32,512]{3,2,1,0:T(8,128)S(1)}, f32[4,2,128,128]{3,2,1,0:T(8,128)S(1)}) custom-call(f32[19,2,32,512]{3,2,1,0:T(8,128)} %pops.1, s32[2,32,512]{2,1,0:T(8,128)} %mask.1, s32[2,512]{1,0:T(2,128)} %wire_hbm.1, f32[4,2,128,128]{3,2,1,0:T(8,128)} %fines.1, f32[4]{0:T(128)} %diff_hbm.1, f32[4]{0:T(128)} %ret_hbm.1), custom_call_target="tpu_custom_call" | custom-call | tf_op jit(solution)/shard_map/drainage/pallas_call | solution.py:622
  59.5 1.7 %put_out.1 = (f32[19,2,32,512]{3,2,1,0:T(8,128)}, f32[4,2,128,128]{3,2,1,0:T(8,128)}) custom-call(f32[19,2,32,512]{3,2,1,0:T(8,128)S(1)} %get-tuple-element.4.a, f32[4,2,128,128]{3,2,1,0:T(8,128)S(1)} %get-tuple-element.5.b), custom_call_target="tpu_custom_call" | custom-call | tf_op jit(solution)/shard_map/put_out/pallas_call | solution.py:603

commit v4 on v3

--- a/solution.py
+++ b/solution.py
@@ -531,7 +531,7 @@
                 from_east = pltpu.roll(east_in, LANES - 1 - n, 1)
                 south = jnp.where(lane == 0, from_west, pltpu.roll(c, 1, 1))
                 north = jnp.where(lane == LANES - 1, from_east, pltpu.roll(c, LANES - 1, 1))
-                X[rows, x * LANES:(x + 1) * LANES] = total([
+                X[0, rows, x * LANES:(x + 1) * LANES] = total([
                     c * (C[0, x, rows, :] - kept * Sall[x, rows, :]),
                     q[s, x, held, :] * C[1, x, rows, :],
                     q[s, x + 2, held, :] * C[2, x, rows, :],
@@ -540,7 +540,7 @@
                     below * C[5, x, rows, :],
                     above * C[6, x, rows, :],
                 ])
-        v = X[...]
+        v = X[0]
         v_hi = v.astype(jnp.bfloat16)
         v_lo = (v - v_hi.astype(jnp.float32)).astype(jnp.bfloat16)
         out = jnp.dot(GB[s], jnp.concatenate([v_hi, v_hi], axis=0), preferred_element_type=jnp.float32)
@@ -552,6 +552,58 @@
             else:
                 fines_out[s, x] = part
 
+    def transport_pair(step, s):
+        q = Q[step]
+        for m in range(2):
+            for x in range(2):
+                q[s + m, x + 1, 7:8, :] = q[s + m, x + 1, 8:9, :]
+                q[s + m, x + 1, 136:137, :] = q[s + m, x + 1, 135:136, :]
+            for c in fine_copies(step, s + m):
+                c.wait_recv()
+        for m in range(2):
+            explicit(step, q, s + m, X.at[m])
+        for m in range(2):
+            out = implicit(s + m, X.at[m])
+            for x in range(2):
+                lanes = out[:, x * LANES:(x + 1) * LANES]
+                if step == 0:
+                    Q1[s + m, x + 1, 8:136, :] = lanes
+                else:
+                    fines_out[s + m, x] = lanes
+
+    def explicit(step, q, s, into):
+        west_in = YW[step, s]
+        east_in = YE[step, s]
+        kept = ret[s]
+        for x in range(2):
+            for zc in range(16):
+                n = x * 16 + zc
+                rows = slice(zc * 8, zc * 8 + 8)
+                held = slice(zc * 8 + 8, zc * 8 + 16)
+                c = q[s, x + 1, held, :]
+                below = q[s, x + 1, zc * 8 + 7:zc * 8 + 15, :]
+                above = q[s, x + 1, zc * 8 + 9:zc * 8 + 17, :]
+                from_west = pltpu.roll(west_in, LANES - n, 1) if n else west_in
+                from_east = pltpu.roll(east_in, LANES - 1 - n, 1)
+                south = jnp.where(lane == 0, from_west, pltpu.roll(c, 1, 1))
+                north = jnp.where(lane == LANES - 1, from_east, pltpu.roll(c, LANES - 1, 1))
+                into[rows, x * LANES:(x + 1) * LANES] = total([
+                    c * (C[0, x, rows, :] - kept * Sall[x, rows, :]),
+                    q[s, x, held, :] * C[1, x, rows, :],
+                    q[s, x + 2, held, :] * C[2, x, rows, :],
+                    south * C[3, x, rows, :],
+                    north * C[4, x, rows, :],
+                    below * C[5, x, rows, :],
+                    above * C[6, x, rows, :],
+                ])
+
+    def implicit(s, values):
+        v = values[...]
+        v_hi = v.astype(jnp.bfloat16)
+        v_lo = (v - v_hi.astype(jnp.float32)).astype(jnp.bfloat16)
+        out = jnp.dot(GB[s], jnp.concatenate([v_hi, v_hi], axis=0), preferred_element_type=jnp.float32)
+        return out + jnp.dot(GB[s, :, 0:LANES], v_lo, preferred_element_type=jnp.float32)
+
     def transport_first(s, _):
         transport(0, s)
         start_planes(1, s)
@@ -562,11 +614,11 @@
     lax.fori_loop(0, 4, transport_first, 0)
     forward_fines(1)
 
-    def transport_second(s, _):
-        transport(1, s)
+    def transport_second(n, _):
+        transport_pair(1, 2 * n)
         return 0
 
-    lax.fori_loop(0, 4, transport_second, 0)
+    lax.fori_loop(0, 2, transport_second, 0)
 
     for s in range(4):
         for c in fine_copies(1, s):
@@ -648,7 +700,7 @@
             pltpu.VMEM((4, 4, 144, LANES), f32),
             pltpu.VMEM((4, 4, 144, LANES), f32),
             pltpu.VMEM((7, 2, 128, LANES), f32),
-            pltpu.VMEM((128, 2 * LANES), f32),
+            pltpu.VMEM((2, 128, 2 * LANES), f32),
             pltpu.VMEM((128, LANES), f32),
             pltpu.VMEM((4, 128, 2 * LANES), jnp.bfloat16),
             pltpu.VMEM((2, 4, 2, 8, LANES), f32),

time: 61.2 us -> 61.2 us (level)
  no operation moved by 1% of the time
where the time goes in v4:
time: 61.2 us; the launch traced here: 61.1 us
  Pallas kernels  60.5 us (99%)
  between operations  0.64 us (1%)
    pallas_call x1, Pallas kernels, on_device(): pl.pallas_call(kernel, out_shape=(jax.ShapeDtypeStruct(populations.shape,...  58.8 us
    pallas_call x1, Pallas kernels, put_out(): pl.pallas_call(put_out_kernel, out_shape=(jax.ShapeDtypeStruct(population...  1.66 us

profile of v4, /device:TPU:32, one launch (start us, length us, event | category | flops | bytes accessed | tf_op | source)
XLA Modules:
  0.0 61.1 jit_solution(11632650382521415662)
XLA Ops:
  0.6 58.8 %drainage.1 = (f32[19,2,32,512]{3,2,1,0:T(8,128)S(1)}, f32[4,2,128,128]{3,2,1,0:T(8,128)S(1)}) custom-call(f32[19,2,32,512]{3,2,1,0:T(8,128)} %pops.1, s32[2,32,512]{2,1,0:T(8,128)} %mask.1, s32[2,512]{1,0:T(2,128)} %wire_hbm.1, f32[4,2,128,128]{3,2,1,0:T(8,128)} %fines.1, f32[4]{0:T(128)} %diff_hbm.1, f32[4]{0:T(128)} %ret_hbm.1), custom_call_target="tpu_custom_call" | custom-call | tf_op jit(solution)/shard_map/drainage/pallas_call | solution.py:674
  59.5 1.7 %put_out.1 = (f32[19,2,32,512]{3,2,1,0:T(8,128)}, f32[4,2,128,128]{3,2,1,0:T(8,128)}) custom-call(f32[19,2,32,512]{3,2,1,0:T(8,128)S(1)} %get-tuple-element.4.a, f32[4,2,128,128]{3,2,1,0:T(8,128)S(1)} %get-tuple-element.5.b), custom_call_target="tpu_custom_call" | custom-call | tf_op jit(solution)/shard_map/put_out/pallas_call | solution.py:655
